TPU v7x, 32 devices: a whole 2x2x4 slice. The times are simulated.
32 devices in a mesh: grp: 2 (over y), dev: 16 (over z, x, core).
Axes of the slice: x: 2, y: 2, z: 4, core: 2. Of those that a mesh axis runs over, the one named last changes fastest.
Arguments:
- queries: float32 [128, 1024], P(('grp', 'dev')), may hold values from -4.5 to 4.5
- documents: float32 [4096, 1024], P(('grp', 'dev')), may hold values from -0.75 to 0.75
- doc_codes: int32 [4096, 128], P(('grp', 'dev')), may hold values from 0 to 255
- codebook: float32 [256, 1024], replicated, may hold values from -0.75 to 0.75
- candidate_owner: int32 [128, 32], P(('grp', 'dev')), may hold values from 0 to 31, all different within a row; in each aligned block of 4 rows (0 to 3, 4 to 7, ...) at most 4 rows name the same one
- candidate_local: int32 [128, 32], P(('grp', 'dev')), may hold values from 0 to 127
Outputs:
- codebook_gradient: float32 [256, 1024], P('dev', 'grp')
- query_loss: float32 [128], P(('grp', 'dev'))
Inputs may be any that keep to these rules, and one draw needn't show every extreme that they name: `candidate_owner`: each query names 32 different owners; among one device's 4 queries no owner is named more than 4 times, and in some device's queries one owner is named exactly 4 times.
All inputs are finite; a program needn't handle non-finite values.
Results may differ from a plain program's by a relative error of at most 0.0003.
Values sent between devices are 32-bit elements; how exact they have to be, the bound alone decides.
No kernel may reach another device: no remote copies, remote signals or barrier semaphores. Data moves between devices by JAX's collectives and lax.ppermute only.
A program may use at most 192 MiB of HBM per device.

v0:
```python
import jax
import jax.numpy as jnp
from jax import lax
from jax.sharding import PartitionSpec as P

D = 1024
M = 128
K = 256
C = 32
SUB = 8


def slot_positions(candidate_owner, capacity):
    owner_flat = candidate_owner.reshape(-1)
    ordinal = jnp.arange(owner_flat.shape[0], dtype=jnp.int32)
    earlier = (owner_flat[None, :] == owner_flat[:, None]) & (ordinal[None, :] < ordinal[:, None])
    rank_inside = jnp.sum(earlier.astype(jnp.int32), axis=1)
    return owner_flat * capacity + rank_inside


def distill(exact_score, student):
    teacher = jax.nn.softmax(exact_score, axis=-1)
    query_loss = jnp.sum(
        teacher * (jax.nn.log_softmax(exact_score, axis=-1) - jax.nn.log_softmax(student, axis=-1)),
        axis=-1,
    )
    weight = jax.nn.softmax(student, axis=-1) - teacher
    return (query_loss, weight)


def code_onehot(code_block):
    return (code_block[:, :, None] == jnp.arange(K, dtype=jnp.int32)[None, None, :]).astype(
        jnp.float32
    )


def fetched_terms(queries, vectors, code_rows, codebook):
    query_count = queries.shape[0]
    exact_score = jnp.einsum("qcd,qd->qc", vectors, queries, precision=lax.Precision.HIGHEST)
    query_parts = queries.reshape(query_count, M, SUB)
    lookup = jnp.einsum(
        "qmj,kmj->qmk", query_parts, codebook.reshape(K, M, SUB), precision=lax.Precision.HIGHEST
    )

    def student_one(pieces):
        code_one, lookup_one = pieces
        return jnp.einsum(
            "cmk,mk->c", code_onehot(code_one), lookup_one, precision=lax.Precision.HIGHEST
        )

    student = lax.map(student_one, (code_rows, lookup))
    query_loss, weight = distill(exact_score, student)

    def table_one(pieces):
        code_one, weight_one = pieces
        return jnp.einsum(
            "cmk,c->mk", code_onehot(code_one), weight_one, precision=lax.Precision.HIGHEST
        )

    weight_table = lax.map(table_one, (code_rows, weight))
    gradient = jnp.einsum(
        "qmk,qmj->kmj", weight_table, query_parts, precision=lax.Precision.HIGHEST
    )
    return (query_loss, gradient.reshape(K, D))


def shards(queries, documents, doc_codes, codebook, candidate_owner, candidate_local):
    groups = lax.axis_size("grp")
    owners = lax.axis_size("dev")
    query_count = queries.shape[0]
    capacity = min(query_count, max(2, 2 * query_count * C // (groups * owners)))
    slot_count = groups * owners * capacity
    positions = slot_positions(candidate_owner, capacity)
    wanted = jnp.zeros((slot_count,), jnp.int32).at[positions].set(candidate_local.reshape(-1))
    asked = lax.all_to_all(
        lax.all_to_all(
            wanted.reshape(groups, owners, capacity), "grp", split_axis=0, concat_axis=0, tiled=True
        ),
        "dev",
        split_axis=1,
        concat_axis=1,
        tiled=True,
    )
    doc_index = asked.reshape(slot_count)
    found_rows = documents[doc_index].reshape(groups, owners, capacity, D)
    found_codes = doc_codes[doc_index].astype(jnp.float32).reshape(groups, owners, capacity, M)
    fetched, fetched_codes = (
        lax.all_to_all(
            lax.all_to_all(found_rows, "grp", split_axis=0, concat_axis=0, tiled=True),
            "dev",
            split_axis=1,
            concat_axis=1,
            tiled=True,
        ),
        lax.all_to_all(
            lax.all_to_all(found_codes, "grp", split_axis=0, concat_axis=0, tiled=True),
            "dev",
            split_axis=1,
            concat_axis=1,
            tiled=True,
        ),
    )
    vectors = fetched.reshape(slot_count, D)[positions].reshape(query_count, C, D)
    code_rows = (
        fetched_codes.reshape(slot_count, M)[positions].astype(jnp.int32).reshape(query_count, C, M)
    )
    query_loss, local_gradient = fetched_terms(queries, vectors, code_rows, codebook)
    partial_sum = lax.psum_scatter(local_gradient, "dev", scatter_dimension=0, tiled=True)
    codebook_gradient = lax.psum_scatter(partial_sum, "grp", scatter_dimension=1, tiled=True)
    return (codebook_gradient, query_loss)


def solution(mesh):
    in_specs = (
        P(("grp", "dev"), None),
        P(("grp", "dev"), None),
        P(("grp", "dev"), None),
        P(),
        P(("grp", "dev"), None),
        P(("grp", "dev"), None),
    )
    out_specs = (P("dev", "grp"), P(("grp", "dev")))
    return jax.shard_map(shards, mesh=mesh, in_specs=in_specs, out_specs=out_specs, check_vma=False)
```

profile of v0, /device:TPU:0, one launch (start us, length us, event | category | flops | bytes accessed | tf_op | source)
XLA Modules:
  0.0 180.2 jit_solution(6461381742338682574)
XLA Ops:
  9.8 1.0 scatter_custom_fusion
  11.0 7.8 %all_to_all.30 = s32[2,16,4]{1,2,0:T(4,128)S(1)} all-to-all(s32[2,16,4]{1,2,0:T(4,128)S(1)} %copy.46), channel_id=1, replica_groups=mesh['grp'=2,'dev'=16] {'grp'}, dimensions={0} | all-to-all | bytes 1024 | tf_op jit(solution)/shard_map/all_to_all | solution.py:76
  18.9 12.2 %all_to_all.31 = s32[2,16,4]{2,0,1:T(2,128)S(1)} all-to-all(s32[2,16,4]{2,0,1:T(2,128)S(1)} %copy.47), channel_id=1, replica_groups=mesh['grp'=2,'dev'=16] {'dev'}, dimensions={1} | all-to-all | bytes 1024 | tf_op jit(solution)/shard_map/all_to_all | solution.py:75
  31.2 1.5 gather_fusion
  32.7 6.5 %all_to_all.32 = f32[2,16,4,128]{3,2,1,0:T(4,128)S(1)} all-to-all(f32[2,16,4,128]{3,2,1,0:T(4,128)S(1)} %bitcast.63), channel_id=1, replica_groups=mesh['grp'=2,'dev'=16] {'grp'}, dimensions={0} | all-to-all | bytes 131072 | tf_op jit(solution)/shard_map/all_to_all | solution.py:96
  39.8 3.5 %all-to-all-start.3 = ((f32[2,16,4,128]{3,2,0,1:T(4,128)}), f32[2,16,4,128]{3,2,0,1:T(4,128)S(1)}, u32[]{:S(2)}, u32[]{:S(2)}) async-start(f32[2,16,4,128]{3,2,0,1:T(4,128)} %copy.49), calls=%async_computation.3 | async-start | bytes 131072 | tf_op jit(solution)/shard_map/all_to_all | solution.py:95
  44.7 1.0 reshape.118
  45.7 4.5 %all-to-all-done.3 = f32[2,16,4,128]{3,2,0,1:T(4,128)S(1)} async-done(((f32[2,16,4,128]{3,2,0,1:T(4,128)}), f32[2,16,4,128]{3,2,0,1:T(4,128)S(1)}, u32[]{:S(2)}, u32[]{:S(2)}) %all-to-all-start.3) | async-done | bytes 65568 | tf_op jit(solution)/shard_map/all_to_all | solution.py:95
  50.2 3.5 %all-to-all-start.4 = ((f32[2,16,4,1024]{3,2,1,0:T(4,128)}), f32[2,16,4,1024]{3,2,1,0:T(4,128)S(1)}, u32[]{:S(2)}, u32[]{:S(2)}) async-start(f32[2,16,4,1024]{3,2,1,0:T(4,128)} %reshape.118), calls=%async_computation.4 | async-start | bytes 1048576 | tf_op jit(solution)/shard_map/all_to_all | solution.py:89
  53.7 1.1 convolution_bitcast_fusion.1
  55.5 6.1 %all-to-all-done.4 = f32[2,16,4,1024]{3,2,1,0:T(4,128)S(1)} async-done(((f32[2,16,4,1024]{3,2,1,0:T(4,128)}), f32[2,16,4,1024]{3,2,1,0:T(4,128)S(1)}, u32[]{:S(2)}, u32[]{:S(2)}) %all-to-all-start.4) | async-done | bytes 524320 | tf_op jit(solution)/shard_map/all_to_all | solution.py:89
  62.5 3.6 %all-to-all-start.5 = ((f32[2,16,4,1024]{3,2,0,1:T(4,128)}), f32[2,16,4,1024]{3,2,0,1:T(4,128)S(1)}, u32[]{:S(2)}, u32[]{:S(2)}) async-start(f32[2,16,4,1024]{3,2,0,1:T(4,128)} %copy.54), calls=%async_computation.5 | async-start | bytes 1048576 | tf_op jit(solution)/shard_map/all_to_all | solution.py:88
  66.1 6.7 %while.20 = (s32[]{:T(128)}, f32[4,32]{1,0:T(4,128)S(1)}, s32[4,32,128]{2,1,0:T(8,128)S(1)}, f32[4,128,256]{2,0,1:T(4,128)S(1)}, s32[]{:T(128)}, /*index=5*/s32[]{:T(128)}) while((s32[]{:T(128)}, f32[4,32]{1,0:T(4,128)S(1)}, s32[4,32,128]{2,1,0:T(8,128)S(1)}, f32[4,128,256]{2,0,1:T(4,128)S(1)}, s32[]{:T(128)}, /*index=5*/s32[]{:T(128)}) %tuple.53), condition=%wide.region_3.4_spmd, body=%wide.region_2.3_spmd.sunk | while | flops 3145698 | bytes 704977 | solution.py:51
  66.3 1.5 select_reduce_fusion.2
  68.0 1.5 select_reduce_fusion.2
  69.7 1.5 select_reduce_fusion.2
  71.4 1.5 select_reduce_fusion.2
  73.0 7.5 %all-to-all-done.5 = f32[2,16,4,1024]{3,2,0,1:T(4,128)S(1)} async-done(((f32[2,16,4,1024]{3,2,0,1:T(4,128)}), f32[2,16,4,1024]{3,2,0,1:T(4,128)S(1)}, u32[]{:S(2)}, u32[]{:S(2)}) %all-to-all-start.5) | async-done | bytes 524320 | tf_op jit(solution)/shard_map/all_to_all | solution.py:88
  83.2 19.7 %while.21 = (s32[]{:T(128)}, f32[4,128,256]{2,0,1:T(4,128)S(1)}, s32[4,32,128]{2,1,0:T(8,128)S(1)}, f32[4,32]{1,0:T(4,128)S(1)}, s32[]{:T(128)}, /*index=5*/s32[]{:T(128)}) while((s32[]{:T(128)}, f32[4,128,256]{2,0,1:T(4,128)S(1)}, s32[4,32,128]{2,1,0:T(8,128)S(1)}, f32[4,32]{1,0:T(4,128)S(1)}, s32[]{:T(128)}, /*index=5*/s32[]{:T(128)}) %tuple.55), condition=%wide.region_9.10_spmd, body=%wide.region_8.9_spmd.sunk | while | flops 13631490 | bytes 2540113 | solution.py:60
  84.1 2.2 %fusion.21 = f32[1,128,256]{2,0,1:T(1,128)S(1)} fusion(pred[32,128,256]{2,1,0:T(32,128)(4,1)S(1)} %iota_compare_fusion.4, f32[4,32]{1,0:T(4,128)S(1)} %get-tuple-element.172, s32[]{:T(128)} %get-tuple-element.163), kind=kOutput, calls=%fused_computation.6.clone.1 | convolution fusion | flops 12582912 | bytes 1180164 | tf_op jit(solution)/shard_map/while/body/eval_jaxpr/cmk,c->mk/dot_general | solution.py:56
  86.2 1.8 %dynamic_update_slice.11 = f32[4,128,256]{2,0,1:T(4,128)S(1)} dynamic-update-slice(f32[4,128,256]{2,0,1:T(4,128)S(1)} %get-tuple-element.164, f32[1,128,256]{2,0,1:T(1,128)S(1)} %fusion.21, s32[]{:T(128)} %get-tuple-element.163, s32[]{:T(128)} %constant.21.clone.1..sunk.1, s32[]{:T(128)} %constant.21.clone.1..sunk.1) | dynamic-update-slice | bytes 262148 | tf_op jit(solution)/shard_map/while/body/jit(dynamic_update_index_in_dim)/dynamic_update_slice | solution.py:60
  88.1 0.9 iota_compare_fusion.4
  89.0 2.2 %fusion.21 = f32[1,128,256]{2,0,1:T(1,128)S(1)} fusion(pred[32,128,256]{2,1,0:T(32,128)(4,1)S(1)} %iota_compare_fusion.4, f32[4,32]{1,0:T(4,128)S(1)} %get-tuple-element.172, s32[]{:T(128)} %get-tuple-element.163), kind=kOutput, calls=%fused_computation.6.clone.1 | convolution fusion | flops 12582912 | bytes 1180164 | tf_op jit(solution)/shard_map/while/body/eval_jaxpr/cmk,c->mk/dot_general | solution.py:56
  91.2 1.8 %dynamic_update_slice.11 = f32[4,128,256]{2,0,1:T(4,128)S(1)} dynamic-update-slice(f32[4,128,256]{2,0,1:T(4,128)S(1)} %get-tuple-element.164, f32[1,128,256]{2,0,1:T(1,128)S(1)} %fusion.21, s32[]{:T(128)} %get-tuple-element.163, s32[]{:T(128)} %constant.21.clone.1..sunk.1, s32[]{:T(128)} %constant.21.clone.1..sunk.1) | dynamic-update-slice | bytes 262148 | tf_op jit(solution)/shard_map/while/body/jit(dynamic_update_index_in_dim)/dynamic_update_slice | solution.py:60
  93.9 2.2 %fusion.21 = f32[1,128,256]{2,0,1:T(1,128)S(1)} fusion(pred[32,128,256]{2,1,0:T(32,128)(4,1)S(1)} %iota_compare_fusion.4, f32[4,32]{1,0:T(4,128)S(1)} %get-tuple-element.172, s32[]{:T(128)} %get-tuple-element.163), kind=kOutput, calls=%fused_computation.6.clone.1 | convolution fusion | flops 12582912 | bytes 1180164 | tf_op jit(solution)/shard_map/while/body/eval_jaxpr/cmk,c->mk/dot_general | solution.py:56
  96.1 1.8 %dynamic_update_slice.11 = f32[4,128,256]{2,0,1:T(4,128)S(1)} dynamic-update-slice(f32[4,128,256]{2,0,1:T(4,128)S(1)} %get-tuple-element.164, f32[1,128,256]{2,0,1:T(1,128)S(1)} %fusion.21, s32[]{:T(128)} %get-tuple-element.163, s32[]{:T(128)} %constant.21.clone.1..sunk.1, s32[]{:T(128)} %constant.21.clone.1..sunk.1) | dynamic-update-slice | bytes 262148 | tf_op jit(solution)/shard_map/while/body/jit(dynamic_update_index_in_dim)/dynamic_update_slice | solution.py:60
  98.9 2.2 %fusion.21 = f32[1,128,256]{2,0,1:T(1,128)S(1)} fusion(pred[32,128,256]{2,1,0:T(32,128)(4,1)S(1)} %iota_compare_fusion.4, f32[4,32]{1,0:T(4,128)S(1)} %get-tuple-element.172, s32[]{:T(128)} %get-tuple-element.163), kind=kOutput, calls=%fused_computation.6.clone.1 | convolution fusion | flops 12582912 | bytes 1180164 | tf_op jit(solution)/shard_map/while/body/eval_jaxpr/cmk,c->mk/dot_general | solution.py:56
  101.0 1.8 %dynamic_update_slice.11 = f32[4,128,256]{2,0,1:T(4,128)S(1)} dynamic-update-slice(f32[4,128,256]{2,0,1:T(4,128)S(1)} %get-tuple-element.164, f32[1,128,256]{2,0,1:T(1,128)S(1)} %fusion.21, s32[]{:T(128)} %get-tuple-element.163, s32[]{:T(128)} %constant.21.clone.1..sunk.1, s32[]{:T(128)} %constant.21.clone.1..sunk.1) | dynamic-update-slice | bytes 262148 | tf_op jit(solution)/shard_map/while/body/jit(dynamic_update_index_in_dim)/dynamic_update_slice | solution.py:60
  102.9 1.4 convolution_bitcast_fusion
  104.3 1.3 copy.58
  105.7 55.9 %reduce-scatter.3.cloned.1.call-done = f32[16,1024]{1,0:T(8,128)} async-done(((f32[256,1024]{1,0:T(8,128)}), f32[16,1024]{1,0:T(8,128)}) %reduce-scatter.3.cloned.1.call-update) | async-done | bytes 65552 | tf_op jit(solution)/shard_map/reduce_scatter | solution.py:108
  161.6 11.7 %reduce-scatter.5.cloned.1.call-done = f32[16,512]{1,0:T(8,128)} async-done(((f32[16,1024]{1,0:T(8,128)}), f32[16,512]{1,0:T(8,128)}) %reduce-scatter.5.cloned.1.call-update) | async-done | bytes 32784 | tf_op jit(solution)/shard_map/reduce_scatter | solution.py:109
  (70 shorter events, 12.6 us)
Async XLA Ops:
  7.2 36.7 %copy-start = (f32[128,1024]{1,0:T(8,128)S(1)}, f32[128,1024]{1,0:T(8,128)}, u32[]{:S(2)}) copy-start(f32[128,1024]{1,0:T(8,128)} %param.12) | copy-start | bytes 1572868
  7.2 36.2 %copy-start.3 = (f32[4,1024]{1,0:T(4,128)S(1)}, f32[4,1024]{1,0:T(4,128)}, u32[]{:S(2)}) copy-start(f32[4,1024]{1,0:T(4,128)} %param.11) | copy-start | bytes 49156
  7.2 36.4 %copy-start.1 = (f32[256,1024]{1,0:T(8,128)S(1)}, f32[256,1024]{1,0:T(8,128)}, u32[]{:S(2)}) copy-start(f32[256,1024]{1,0:T(8,128)} %param.14) | copy-start | bytes 3145732
  39.8 10.4 %all-to-all-start.3 = ((f32[2,16,4,128]{3,2,0,1:T(4,128)}), f32[2,16,4,128]{3,2,0,1:T(4,128)S(1)}, u32[]{:S(2)}, u32[]{:S(2)}) async-start(f32[2,16,4,128]{3,2,0,1:T(4,128)} %copy.49), calls=%async_computation.3 | async-start | bytes 131072 | tf_op jit(solution)/shard_map/all_to_all | solution.py:95
  50.2 11.5 %all-to-all-start.4 = ((f32[2,16,4,1024]{3,2,1,0:T(4,128)}), f32[2,16,4,1024]{3,2,1,0:T(4,128)S(1)}, u32[]{:S(2)}, u32[]{:S(2)}) async-start(f32[2,16,4,1024]{3,2,1,0:T(4,128)} %reshape.118), calls=%async_computation.4 | async-start | bytes 1048576 | tf_op jit(solution)/shard_map/all_to_all | solution.py:89
  62.5 18.0 %all-to-all-start.5 = ((f32[2,16,4,1024]{3,2,0,1:T(4,128)}), f32[2,16,4,1024]{3,2,0,1:T(4,128)S(1)}, u32[]{:S(2)}, u32[]{:S(2)}) async-start(f32[2,16,4,1024]{3,2,0,1:T(4,128)} %copy.54), calls=%async_computation.5 | async-start | bytes 1048576 | tf_op jit(solution)/shard_map/all_to_all | solution.py:88
  66.1 95.5 %reduce-scatter.3.cloned.1.call-start = ((), (), s32[]{:S(2)}) async-start(), calls=%async_computation.8 | async-start | bytes 1114112 | tf_op jit(solution)/shard_map/reduce_scatter | solution.py:108
  80.7 2.5 %copy-start.2 = (f32[4,128,256]{2,0,1:T(4,128)S(1)}, f32[4,128,256]{2,0,1:T(4,128)}, u32[]{:S(2)}) copy-start(f32[4,128,256]{2,0,1:T(4,128)} %custom-call.9) | copy-start | bytes 1572868
  105.6 67.8 %reduce-scatter.5.cloned.1.call-start = ((), (), s32[]{:S(2)}) async-start(), calls=%async_computation.9 | async-start | bytes 98304 | tf_op jit(solution)/shard_map/reduce_scatter | solution.py:109
Sparse Core Ops, SparseCore 0:
  105.7 55.8 reduce-scatter.2
  164.5 8.8 reduce-scatter.4
where the time goes:
time: 181 us; the launch traced here: 180 us
  waiting for transfers between devices  85.9 us (47%)
  blocking collectives  26.5 us (15%)
  local copies, waits for them, and re-layouts  19.3 us (11%)
  between operations  14.3 us (8%)
  matrix products  11.8 us (7%)
  other arithmetic  11.6 us (6%)
  starting transfers between devices  10.6 us (6%)
    reduce_scatter x1, waiting for transfers between devices, shards(): lax.psum_scatter(local_gradient, 'dev', scatter_dimension=0, tiled=True)  55.9 us
    all_to_all x1, blocking collectives, shards(): lax.all_to_all(lax.all_to_all(wanted.reshape(groups, owners, capacity), '...  12.2 us
    reduce_scatter x1, waiting for transfers between devices, shards(): lax.psum_scatter(partial_sum, 'grp', scatter_dimension=1, tiled=True)  11.7 us
    dot_general x4, matrix products, table_one(): jnp.einsum('cmk,c->mk', code_onehot(code_one), weight_one, precision=lax....  8.72 us
    all_to_all x1, blocking collectives, shards(): lax.all_to_all(wanted.reshape(groups, owners, capacity), 'grp', split_axi...  7.82 us
    all_to_all x1, waiting for transfers between devices, shards(): lax.all_to_all(lax.all_to_all(found_rows, 'grp', split_axis=0, concat_axi...  7.51 us
    dynamic_update_slice x4, local copies, waits for them, and re-layouts, fetched_terms(): weight_table = lax.map(table_one, (code_rows, weight))  7.34 us
    all_to_all x1, blocking collectives, shards(): lax.all_to_all(found_codes, 'grp', split_axis=0, concat_axis=0, tiled=True)  6.5 us
  transfers between devices with their start and end apart: 5, of which 5 were waited for; matrix products, arithmetic and copies ran while one was open for 6% of the time, Pallas kernels for 0%

commit v1 on v0

--- a/solution.py
+++ b/solution.py
@@ -8,6 +8,22 @@
 K = 256
 C = 32
 SUB = 8
+
+
+def swapped_with_each(x, axis, split, join):
+    ways, here = (lax.axis_size(axis), lax.axis_index(axis))
+    width = x.shape[split] // ways
+    dims = list(x.shape)
+    dims[split] = width
+    height = dims[join]
+    dims[join] = height * ways
+    full = jnp.zeros(dims, x.dtype)
+    for mask in range(ways):
+        part = lax.dynamic_slice_in_dim(x, (here ^ mask) * width, width, axis=split)
+        if mask:
+            part = lax.ppermute(part, axis, [(d, d ^ mask) for d in range(ways)])
+        full = lax.dynamic_update_slice_in_dim(full, part, (here ^ mask) * height, axis=join)
+    return full
 
 
 def slot_positions(candidate_owner, capacity):
@@ -92,12 +108,8 @@
             concat_axis=1,
             tiled=True,
         ),
-        lax.all_to_all(
-            lax.all_to_all(found_codes, "grp", split_axis=0, concat_axis=0, tiled=True),
-            "dev",
-            split_axis=1,
-            concat_axis=1,
-            tiled=True,
+        swapped_with_each(
+            lax.all_to_all(found_codes, "grp", split_axis=0, concat_axis=0, tiled=True), "dev", 1, 1
         ),
     )
     vectors = fetched.reshape(slot_count, D)[positions].reshape(query_count, C, D)

time: 181 us -> 192 us (1.061)
  starting transfers between devices: 10.6 us -> 38.8 us
  blocking collectives: 26.5 us -> 7.82 us
    ppermute x0 -> x15, starting transfers between devices: none -> 20.5 us  [swapped_with_each(): part = lax.ppermute(part, axis, [(d, d ^ mask) for d in range(ways)])]
    all_to_all x2 -> x0, blocking collectives: 18.7 us -> none  [the longest x1 12.2 us: shards(): lax.all_to_all(lax.all_to_all(wanted.reshape(groups, owners, capacity), '...]
    all_to_all x1, waiting for transfers between devices: 6.14 us -> 0.01 us  [shards(): lax.all_to_all(found_rows, 'grp', split_axis=0, concat_axis=0, tiled=True)]
    all_to_all x1 -> x2, starting transfers between devices: 3.49 us -> 9.2 us  [the longest x1 5.91 us: shards(): lax.all_to_all(lax.all_to_all(wanted.reshape(groups, owners, capacity), '...]
    all_to_all x1 -> x2, waiting for transfers between devices: 4.53 us -> 6.87 us  [the longest x1 4 us: shards(): lax.all_to_all(lax.all_to_all(wanted.reshape(groups, owners, capacity), '...]
  transfers between devices with their start and end apart: 5 -> 21, of which waited for: 5 -> 7; matrix products, arithmetic and copies ran while one was open for 6% -> 7% of each run, Pallas kernels for 0% -> 0%
where the time goes in v1:
time: 192 us; the launch traced here: 191 us
  waiting for transfers between devices  85.4 us (44%)
  starting transfers between devices  38.8 us (20%)
  local copies, waits for them, and re-layouts  20.5 us (11%)
  between operations  14.4 us (8%)
  other arithmetic  12.2 us (6%)
  matrix products  11.8 us (6%)
  blocking collectives  7.82 us (4%)
    reduce_scatter x1, waiting for transfers between devices, shards(): lax.psum_scatter(local_gradient, 'dev', scatter_dimension=0, tiled=True)  57.4 us
    ppermute x15, starting transfers between devices, swapped_with_each(): part = lax.ppermute(part, axis, [(d, d ^ mask) for d in range(ways)])  20.5 us
    reduce_scatter x1, waiting for transfers between devices, shards(): lax.psum_scatter(partial_sum, 'grp', scatter_dimension=1, tiled=True)  11.7 us
    dot_general x4, matrix products, table_one(): jnp.einsum('cmk,c->mk', code_onehot(code_one), weight_one, precision=lax....  8.72 us
    all_to_all x1, blocking collectives, shards(): lax.all_to_all(wanted.reshape(groups, owners, capacity), 'grp', split_axi...  7.82 us
    all_to_all x1, waiting for transfers between devices, shards(): lax.all_to_all(lax.all_to_all(found_rows, 'grp', split_axis=0, concat_axi...  7.56 us
    dynamic_update_slice x4, local copies, waits for them, and re-layouts, fetched_terms(): weight_table = lax.map(table_one, (code_rows, weight))  7.34 us
    dot_general x4, other arithmetic, student_one(): jnp.einsum('cmk,mk->c', code_onehot(code_one), lookup_one, precision=lax....  5.94 us
  transfers between devices with their start and end apart: 21, of which 7 were waited for; matrix products, arithmetic and copies ran while one was open for 7% of the time, Pallas kernels for 0%

profile of v1, /device:TPU:0, one launch (start us, length us, event | category | flops | bytes accessed | tf_op | source)
XLA Modules:
  0.0 191.1 jit_solution(11485682397129573600)
XLA Ops:
  10.9 7.8 %all_to_all.25 = s32[2,16,4]{1,2,0:T(4,128)S(1)} all-to-all(s32[2,16,4]{1,2,0:T(4,128)S(1)} %copy.42), channel_id=1, replica_groups=mesh['grp'=2,'dev'=16] {'grp'}, dimensions={0} | all-to-all | bytes 1024 | tf_op jit(solution)/shard_map/all_to_all | solution.py:92
  19.4 5.9 %all-to-all-start.1 = ((s32[2,16,4]{2,0,1:T(2,128)}), s32[2,16,4]{2,0,1:T(2,128)S(1)}, u32[]{:S(2)}, u32[]{:S(2)}) async-start(s32[2,16,4]{2,0,1:T(2,128)} %copy.43), calls=%async_computation.1 | async-start | bytes 32768 | tf_op jit(solution)/shard_map/all_to_all | solution.py:91
  26.2 1.6 copy.45
  27.8 4.0 %all-to-all-done.1 = s32[2,16,4]{2,0,1:T(2,128)S(1)} async-done(((s32[2,16,4]{2,0,1:T(2,128)}), s32[2,16,4]{2,0,1:T(2,128)S(1)}, u32[]{:S(2)}, u32[]{:S(2)}) %all-to-all-start.1) | async-done | bytes 544 | tf_op jit(solution)/shard_map/all_to_all | solution.py:91
  33.3 3.3 %all-to-all-start.2 = ((f32[2,16,4,128]{3,2,1,0:T(4,128)}), f32[2,16,4,128]{3,2,1,0:T(4,128)S(1)}, u32[]{:S(2)}, u32[]{:S(2)}) async-start(f32[2,16,4,128]{3,2,1,0:T(4,128)} %bitcast.13), calls=%async_computation.2 | async-start | bytes 131072 | tf_op jit(solution)/shard_map/all_to_all | solution.py:112
  37.8 2.9 %all-to-all-done.2 = f32[2,16,4,128]{3,2,1,0:T(4,128)S(1)} async-done(((f32[2,16,4,128]{3,2,1,0:T(4,128)}), f32[2,16,4,128]{3,2,1,0:T(4,128)S(1)}, u32[]{:S(2)}, u32[]{:S(2)}) %all-to-all-start.2) | async-done | bytes 65568 | tf_op jit(solution)/shard_map/all_to_all | solution.py:112
  42.6 3.5 %all-to-all-start.3 = ((f32[2,16,4,1024]{3,2,1,0:T(4,128)}), f32[2,16,4,1024]{3,2,1,0:T(4,128)S(1)}, u32[]{:S(2)}, u32[]{:S(2)}) async-start(f32[2,16,4,1024]{3,2,1,0:T(4,128)} %reshape.118), calls=%async_computation.3 | async-start | bytes 1048576 | tf_op jit(solution)/shard_map/all_to_all | solution.py:105
  46.7 1.4 collective-permute-start.2
  50.2 2.2 %collective-permute-start.6 = (f32[2,1,4,128]{3,2,1,0:T(4,128)S(1)}, f32[2,1,4,128]{3,2,1,0:T(4,128)S(1)}, u32[]{:S(2)}, u32[]{:S(2)}) collective-permute-start(f32[2,1,4,128]{3,2,1,0:T(4,128)S(1)} %get-tuple-element.93), channel_id=1, source_target_pairs={{0,7},{1,6},{2,5},{3,4},{4,3},{5,2},{6,1},{7,0},{8,15},{9,14},{10,... | collective-permute-start | bytes 12296 | tf_op jit(solution)/shard_map/ppermute | solution.py:24
  52.9 2.1 %collective-permute-start.8 = (f32[2,1,4,128]{3,2,1,0:T(4,128)S(1)}, f32[2,1,4,128]{3,2,1,0:T(4,128)S(1)}, u32[]{:S(2)}, u32[]{:S(2)}) collective-permute-start(f32[2,1,4,128]{3,2,1,0:T(4,128)S(1)} %get-tuple-element.91), channel_id=1, source_target_pairs={{0,9},{1,8},{2,11},{3,10},{4,13},{5,12},{6,15},{7,14},{8,1},{9,0},... | collective-permute-start | bytes 12296 | tf_op jit(solution)/shard_map/ppermute | solution.py:24
  55.6 3.1 %collective-permute-start.10 = (f32[2,1,4,128]{3,2,1,0:T(4,128)S(1)}, f32[2,1,4,128]{3,2,1,0:T(4,128)S(1)}, u32[]{:S(2)}, u32[]{:S(2)}) collective-permute-start(f32[2,1,4,128]{3,2,1,0:T(4,128)S(1)} %get-tuple-element.89), channel_id=1, source_target_pairs={{0,11},{1,10},{2,9},{3,8},{4,15},{5,14},{6,13},{7,12},{8,3},{9,2},... | collective-permute-start | bytes 12296 | tf_op jit(solution)/shard_map/ppermute | solution.py:24
  59.2 3.0 %collective-permute-start.12 = (f32[2,1,4,128]{3,2,1,0:T(4,128)S(1)}, f32[2,1,4,128]{3,2,1,0:T(4,128)S(1)}, u32[]{:S(2)}, u32[]{:S(2)}) collective-permute-start(f32[2,1,4,128]{3,2,1,0:T(4,128)S(1)} %get-tuple-element.87), channel_id=1, source_target_pairs={{0,13},{1,12},{2,15},{3,14},{4,9},{5,8},{6,11},{7,10},{8,5},{9,4},... | collective-permute-start | bytes 12296 | tf_op jit(solution)/shard_map/ppermute | solution.py:24
  62.8 3.9 %collective-permute-start.14 = (f32[2,1,4,128]{3,2,1,0:T(4,128)S(1)}, f32[2,1,4,128]{3,2,1,0:T(4,128)S(1)}, u32[]{:S(2)}, u32[]{:S(2)}) collective-permute-start(f32[2,1,4,128]{3,2,1,0:T(4,128)S(1)} %get-tuple-element.85), channel_id=1, source_target_pairs={{0,15},{1,14},{2,13},{3,12},{4,11},{5,10},{6,9},{7,8},{8,7},{9,6},... | collective-permute-start | bytes 12296 | tf_op jit(solution)/shard_map/ppermute | solution.py:24
  66.8 1.7 collective-permute-done.13
  70.1 5.5 %all-to-all-start.4 = ((f32[2,16,4,1024]{3,2,0,1:T(4,128)}), f32[2,16,4,1024]{3,2,0,1:T(4,128)S(1)}, u32[]{:S(2)}, u32[]{:S(2)}) async-start(f32[2,16,4,1024]{3,2,0,1:T(4,128)} %copy.48), calls=%async_computation.4 | async-start | bytes 1048576 | tf_op jit(solution)/shard_map/all_to_all | solution.py:104
  75.6 6.7 %while.20 = (s32[]{:T(128)}, f32[4,32]{1,0:T(4,128)S(1)}, s32[4,32,128]{2,1,0:T(8,128)S(1)}, f32[4,128,256]{2,0,1:T(4,128)S(1)}, s32[]{:T(128)}, /*index=5*/s32[]{:T(128)}) while((s32[]{:T(128)}, f32[4,32]{1,0:T(4,128)S(1)}, s32[4,32,128]{2,1,0:T(8,128)S(1)}, f32[4,128,256]{2,0,1:T(4,128)S(1)}, s32[]{:T(128)}, /*index=5*/s32[]{:T(128)}) %tuple.68), condition=%wide.region_3.4_spmd, body=%wide.region_2.3_spmd.sunk | while | flops 3145698 | bytes 704977 | solution.py:67
  75.8 1.5 select_reduce_fusion.2
  77.5 1.5 select_reduce_fusion.2
  79.1 1.5 select_reduce_fusion.2
  80.8 1.5 select_reduce_fusion.2
  82.5 7.6 %all-to-all-done.4 = f32[2,16,4,1024]{3,2,0,1:T(4,128)S(1)} async-done(((f32[2,16,4,1024]{3,2,0,1:T(4,128)}), f32[2,16,4,1024]{3,2,0,1:T(4,128)S(1)}, u32[]{:S(2)}, u32[]{:S(2)}) %all-to-all-start.4) | async-done | bytes 524320 | tf_op jit(solution)/shard_map/all_to_all | solution.py:104
  92.7 19.7 %while.21 = (s32[]{:T(128)}, f32[4,128,256]{2,0,1:T(4,128)S(1)}, s32[4,32,128]{2,1,0:T(8,128)S(1)}, f32[4,32]{1,0:T(4,128)S(1)}, s32[]{:T(128)}, /*index=5*/s32[]{:T(128)}) while((s32[]{:T(128)}, f32[4,128,256]{2,0,1:T(4,128)S(1)}, s32[4,32,128]{2,1,0:T(8,128)S(1)}, f32[4,32]{1,0:T(4,128)S(1)}, s32[]{:T(128)}, /*index=5*/s32[]{:T(128)}) %tuple.69), condition=%wide.region_9.10_spmd, body=%wide.region_8.9_spmd.sunk | while | flops 13631490 | bytes 2540113 | solution.py:76
  93.6 2.2 %fusion.21 = f32[1,128,256]{2,0,1:T(1,128)S(1)} fusion(pred[32,128,256]{2,1,0:T(32,128)(4,1)S(1)} %iota_compare_fusion.4, f32[4,32]{1,0:T(4,128)S(1)} %get-tuple-element.188, s32[]{:T(128)} %get-tuple-element.179), kind=kOutput, calls=%fused_computation.6.clone.1 | convolution fusion | flops 12582912 | bytes 1180164 | tf_op jit(solution)/shard_map/while/body/eval_jaxpr/cmk,c->mk/dot_general | solution.py:72
  95.8 1.8 dynamic_update_slice.91
  98.5 2.2 %fusion.21 = f32[1,128,256]{2,0,1:T(1,128)S(1)} fusion(pred[32,128,256]{2,1,0:T(32,128)(4,1)S(1)} %iota_compare_fusion.4, f32[4,32]{1,0:T(4,128)S(1)} %get-tuple-element.188, s32[]{:T(128)} %get-tuple-element.179), kind=kOutput, calls=%fused_computation.6.clone.1 | convolution fusion | flops 12582912 | bytes 1180164 | tf_op jit(solution)/shard_map/while/body/eval_jaxpr/cmk,c->mk/dot_general | solution.py:72
  100.7 1.8 dynamic_update_slice.91
  103.5 2.2 %fusion.21 = f32[1,128,256]{2,0,1:T(1,128)S(1)} fusion(pred[32,128,256]{2,1,0:T(32,128)(4,1)S(1)} %iota_compare_fusion.4, f32[4,32]{1,0:T(4,128)S(1)} %get-tuple-element.188, s32[]{:T(128)} %get-tuple-element.179), kind=kOutput, calls=%fused_computation.6.clone.1 | convolution fusion | flops 12582912 | bytes 1180164 | tf_op jit(solution)/shard_map/while/body/eval_jaxpr/cmk,c->mk/dot_general | solution.py:72
  105.6 1.8 dynamic_update_slice.91
  108.4 2.2 %fusion.21 = f32[1,128,256]{2,0,1:T(1,128)S(1)} fusion(pred[32,128,256]{2,1,0:T(32,128)(4,1)S(1)} %iota_compare_fusion.4, f32[4,32]{1,0:T(4,128)S(1)} %get-tuple-element.188, s32[]{:T(128)} %get-tuple-element.179), kind=kOutput, calls=%fused_computation.6.clone.1 | convolution fusion | flops 12582912 | bytes 1180164 | tf_op jit(solution)/shard_map/while/body/eval_jaxpr/cmk,c->mk/dot_general | solution.py:72
  110.6 1.8 dynamic_update_slice.91
  115.2 57.4 %reduce-scatter.3.cloned.1.call-done = f32[16,1024]{1,0:T(8,128)} async-done(((f32[256,1024]{1,0:T(8,128)}), f32[16,1024]{1,0:T(8,128)}) %reduce-scatter.3.cloned.1.call-update) | async-done | bytes 65552 | tf_op jit(solution)/shard_map/reduce_scatter | solution.py:120
  172.6 11.7 %reduce-scatter.5.cloned.1.call-done = f32[16,512]{1,0:T(8,128)} async-done(((f32[16,1024]{1,0:T(8,128)}), f32[16,512]{1,0:T(8,128)}) %reduce-scatter.5.cloned.1.call-update) | async-done | bytes 32784 | tf_op jit(solution)/shard_map/reduce_scatter | solution.py:121
  (113 shorter events, 26.0 us)
Async XLA Ops:
  7.2 33.7 %copy-start = (f32[128,1024]{1,0:T(8,128)S(1)}, f32[128,1024]{1,0:T(8,128)}, u32[]{:S(2)}) copy-start(f32[128,1024]{1,0:T(8,128)} %param.12) | copy-start | bytes 1572868
  19.4 12.4 %all-to-all-start.1 = ((s32[2,16,4]{2,0,1:T(2,128)}), s32[2,16,4]{2,0,1:T(2,128)S(1)}, u32[]{:S(2)}, u32[]{:S(2)}) async-start(s32[2,16,4]{2,0,1:T(2,128)} %copy.43), calls=%async_computation.1 | async-start | bytes 32768 | tf_op jit(solution)/shard_map/all_to_all | solution.py:91
  26.2 5.7 %copy-start.1 = (s32[128,128]{1,0:T(8,128)S(1)}, s32[128,128]{1,0:T(8,128)}, u32[]{:S(2)}) copy-start(s32[128,128]{1,0:T(8,128)} %param.13) | copy-start | bytes 196612
  33.3 7.4 %all-to-all-start.2 = ((f32[2,16,4,128]{3,2,1,0:T(4,128)}), f32[2,16,4,128]{3,2,1,0:T(4,128)S(1)}, u32[]{:S(2)}, u32[]{:S(2)}) async-start(f32[2,16,4,128]{3,2,1,0:T(4,128)} %bitcast.13), calls=%async_computation.2 | async-start | bytes 131072 | tf_op jit(solution)/shard_map/all_to_all | solution.py:112
  40.8 8.9 %collective-permute-start = (f32[2,1,4,128]{3,2,1,0:T(4,128)S(1)}, f32[2,1,4,128]{3,2,1,0:T(4,128)S(1)}, u32[]{:S(2)}, u32[]{:S(2)}) collective-permute-start(f32[2,1,4,128]{3,2,1,0:T(4,128)S(1)} %get-tuple-element.99), channel_id=1, source_target_pairs={{0,1},{1,0},{2,3},{3,2},{4,5},{5,4},{6,7},{7,6},{8,9},{9,8},{10,11... | collective-permute-start | bytes 12296 | tf_op jit(solution)/shard_map/ppermute | solution.py:24
  42.6 26.6 %all-to-all-start.3 = ((f32[2,16,4,1024]{3,2,1,0:T(4,128)}), f32[2,16,4,1024]{3,2,1,0:T(4,128)S(1)}, u32[]{:S(2)}, u32[]{:S(2)}) async-start(f32[2,16,4,1024]{3,2,1,0:T(4,128)} %reshape.118), calls=%async_computation.3 | async-start | bytes 1048576 | tf_op jit(solution)/shard_map/all_to_all | solution.py:105
  46.1 4.0 %collective-permute-start.1 = (f32[2,1,4,128]{3,2,1,0:T(4,128)S(1)}, f32[2,1,4,128]{3,2,1,0:T(4,128)S(1)}, u32[]{:S(2)}, u32[]{:S(2)}) collective-permute-start(f32[2,1,4,128]{3,2,1,0:T(4,128)S(1)} %get-tuple-element.98), channel_id=1, source_target_pairs={{0,2},{1,3},{2,0},{3,1},{4,6},{5,7},{6,4},{7,5},{8,10},{9,11},{10,... | collective-permute-start | bytes 12296 | tf_op jit(solution)/shard_map/ppermute | solution.py:24
  46.7 5.8 %collective-permute-start.2 = (f32[2,1,4,128]{3,2,1,0:T(4,128)S(1)}, f32[2,1,4,128]{3,2,1,0:T(4,128)S(1)}, u32[]{:S(2)}, u32[]{:S(2)}) collective-permute-start(f32[2,1,4,128]{3,2,1,0:T(4,128)S(1)} %get-tuple-element.97), channel_id=1, source_target_pairs={{0,3},{1,2},{2,1},{3,0},{4,7},{5,6},{6,5},{7,4},{8,11},{9,10},{10,... | collective-permute-start | bytes 12296 | tf_op jit(solution)/shard_map/ppermute | solution.py:24
  48.0 4.9 %collective-permute-start.3 = (f32[2,1,4,128]{3,2,1,0:T(4,128)S(1)}, f32[2,1,4,128]{3,2,1,0:T(4,128)S(1)}, u32[]{:S(2)}, u32[]{:S(2)}) collective-permute-start(f32[2,1,4,128]{3,2,1,0:T(4,128)S(1)} %get-tuple-element.96), channel_id=1, source_target_pairs={{0,4},{1,5},{2,6},{3,7},{4,0},{5,1},{6,2},{7,3},{8,12},{9,13},{10,... | collective-permute-start | bytes 12296 | tf_op jit(solution)/shard_map/ppermute | solution.py:24
  48.5 6.6 %collective-permute-start.4 = (f32[2,1,4,128]{3,2,1,0:T(4,128)S(1)}, f32[2,1,4,128]{3,2,1,0:T(4,128)S(1)}, u32[]{:S(2)}, u32[]{:S(2)}) collective-permute-start(f32[2,1,4,128]{3,2,1,0:T(4,128)S(1)} %get-tuple-element.95), channel_id=1, source_target_pairs={{0,5},{1,4},{2,7},{3,6},{4,1},{5,0},{6,3},{7,2},{8,13},{9,12},{10,... | collective-permute-start | bytes 12296 | tf_op jit(solution)/shard_map/ppermute | solution.py:24
  49.7 5.8 %collective-permute-start.5 = (f32[2,1,4,128]{3,2,1,0:T(4,128)S(1)}, f32[2,1,4,128]{3,2,1,0:T(4,128)S(1)}, u32[]{:S(2)}, u32[]{:S(2)}) collective-permute-start(f32[2,1,4,128]{3,2,1,0:T(4,128)S(1)} %get-tuple-element.94), channel_id=1, source_target_pairs={{0,6},{1,7},{2,4},{3,5},{4,2},{5,3},{6,0},{7,1},{8,14},{9,15},{10,... | collective-permute-start | bytes 12296 | tf_op jit(solution)/shard_map/ppermute | solution.py:24
  50.2 8.5 %collective-permute-start.6 = (f32[2,1,4,128]{3,2,1,0:T(4,128)S(1)}, f32[2,1,4,128]{3,2,1,0:T(4,128)S(1)}, u32[]{:S(2)}, u32[]{:S(2)}) collective-permute-start(f32[2,1,4,128]{3,2,1,0:T(4,128)S(1)} %get-tuple-element.93), channel_id=1, source_target_pairs={{0,7},{1,6},{2,5},{3,4},{4,3},{5,2},{6,1},{7,0},{8,15},{9,14},{10,... | collective-permute-start | bytes 12296 | tf_op jit(solution)/shard_map/ppermute | solution.py:24
  52.4 6.8 %collective-permute-start.7 = (f32[2,1,4,128]{3,2,1,0:T(4,128)S(1)}, f32[2,1,4,128]{3,2,1,0:T(4,128)S(1)}, u32[]{:S(2)}, u32[]{:S(2)}) collective-permute-start(f32[2,1,4,128]{3,2,1,0:T(4,128)S(1)} %get-tuple-element.92), channel_id=1, source_target_pairs={{0,8},{1,9},{2,10},{3,11},{4,12},{5,13},{6,14},{7,15},{8,0},{9,1},... | collective-permute-start | bytes 12296 | tf_op jit(solution)/shard_map/ppermute | solution.py:24
  52.9 9.2 %collective-permute-start.8 = (f32[2,1,4,128]{3,2,1,0:T(4,128)S(1)}, f32[2,1,4,128]{3,2,1,0:T(4,128)S(1)}, u32[]{:S(2)}, u32[]{:S(2)}) collective-permute-start(f32[2,1,4,128]{3,2,1,0:T(4,128)S(1)} %get-tuple-element.91), channel_id=1, source_target_pairs={{0,9},{1,8},{2,11},{3,10},{4,13},{5,12},{6,15},{7,14},{8,1},{9,0},... | collective-permute-start | bytes 12296 | tf_op jit(solution)/shard_map/ppermute | solution.py:24
  55.0 7.8 %collective-permute-start.9 = (f32[2,1,4,128]{3,2,1,0:T(4,128)S(1)}, f32[2,1,4,128]{3,2,1,0:T(4,128)S(1)}, u32[]{:S(2)}, u32[]{:S(2)}) collective-permute-start(f32[2,1,4,128]{3,2,1,0:T(4,128)S(1)} %get-tuple-element.90), channel_id=1, source_target_pairs={{0,10},{1,11},{2,8},{3,9},{4,14},{5,15},{6,12},{7,13},{8,2},{9,3},... | collective-permute-start | bytes 12296 | tf_op jit(solution)/shard_map/ppermute | solution.py:24
  55.6 11.2 %collective-permute-start.10 = (f32[2,1,4,128]{3,2,1,0:T(4,128)S(1)}, f32[2,1,4,128]{3,2,1,0:T(4,128)S(1)}, u32[]{:S(2)}, u32[]{:S(2)}) collective-permute-start(f32[2,1,4,128]{3,2,1,0:T(4,128)S(1)} %get-tuple-element.89), channel_id=1, source_target_pairs={{0,11},{1,10},{2,9},{3,8},{4,15},{5,14},{6,13},{7,12},{8,3},{9,2},... | collective-permute-start | bytes 12296 | tf_op jit(solution)/shard_map/ppermute | solution.py:24
  58.7 8.0 %collective-permute-start.11 = (f32[2,1,4,128]{3,2,1,0:T(4,128)S(1)}, f32[2,1,4,128]{3,2,1,0:T(4,128)S(1)}, u32[]{:S(2)}, u32[]{:S(2)}) collective-permute-start(f32[2,1,4,128]{3,2,1,0:T(4,128)S(1)} %get-tuple-element.88), channel_id=1, source_target_pairs={{0,12},{1,13},{2,14},{3,15},{4,8},{5,9},{6,10},{7,11},{8,4},{9,5},... | collective-permute-start | bytes 12296 | tf_op jit(solution)/shard_map/ppermute | solution.py:24
  59.2 7.5 %collective-permute-start.12 = (f32[2,1,4,128]{3,2,1,0:T(4,128)S(1)}, f32[2,1,4,128]{3,2,1,0:T(4,128)S(1)}, u32[]{:S(2)}, u32[]{:S(2)}) collective-permute-start(f32[2,1,4,128]{3,2,1,0:T(4,128)S(1)} %get-tuple-element.87), channel_id=1, source_target_pairs={{0,13},{1,12},{2,15},{3,14},{4,9},{5,8},{6,11},{7,10},{8,5},{9,4},... | collective-permute-start | bytes 12296 | tf_op jit(solution)/shard_map/ppermute | solution.py:24
  62.2 6.3 %collective-permute-start.13 = (f32[2,1,4,128]{3,2,1,0:T(4,128)S(1)}, f32[2,1,4,128]{3,2,1,0:T(4,128)S(1)}, u32[]{:S(2)}, u32[]{:S(2)}) collective-permute-start(f32[2,1,4,128]{3,2,1,0:T(4,128)S(1)} %get-tuple-element.86), channel_id=1, source_target_pairs={{0,14},{1,15},{2,12},{3,13},{4,10},{5,11},{6,8},{7,9},{8,6},{9,7},... | collective-permute-start | bytes 12296 | tf_op jit(solution)/shard_map/ppermute | solution.py:24
  62.8 5.7 %collective-permute-start.14 = (f32[2,1,4,128]{3,2,1,0:T(4,128)S(1)}, f32[2,1,4,128]{3,2,1,0:T(4,128)S(1)}, u32[]{:S(2)}, u32[]{:S(2)}) collective-permute-start(f32[2,1,4,128]{3,2,1,0:T(4,128)S(1)} %get-tuple-element.85), channel_id=1, source_target_pairs={{0,15},{1,14},{2,13},{3,12},{4,11},{5,10},{6,9},{7,8},{8,7},{9,6},... | collective-permute-start | bytes 12296 | tf_op jit(solution)/shard_map/ppermute | solution.py:24
  70.1 19.9 %all-to-all-start.4 = ((f32[2,16,4,1024]{3,2,0,1:T(4,128)}), f32[2,16,4,1024]{3,2,0,1:T(4,128)S(1)}, u32[]{:S(2)}, u32[]{:S(2)}) async-start(f32[2,16,4,1024]{3,2,0,1:T(4,128)} %copy.48), calls=%async_computation.4 | async-start | bytes 1048576 | tf_op jit(solution)/shard_map/all_to_all | solution.py:104
  75.6 97.0 %reduce-scatter.3.cloned.1.call-start = ((), (), s32[]{:S(2)}) async-start(), calls=%async_computation.7 | async-start | bytes 1114112 | tf_op jit(solution)/shard_map/reduce_scatter | solution.py:120
  90.3 0.8 copy-start.2
  115.1 69.2 %reduce-scatter.5.cloned.1.call-start = ((), (), s32[]{:S(2)}) async-start(), calls=%async_computation.8 | async-start | bytes 98304 | tf_op jit(solution)/shard_map/reduce_scatter | solution.py:121
Sparse Core Ops, SparseCore 0:
  115.2 57.2 reduce-scatter.2
  175.4 8.8 reduce-scatter.4
